TPU v7x, 32 devices: a whole 2x2x4 slice. The times are simulated.
32 devices in a mesh: aux: 8 (over z, x), pair: 4 (over y, core).
Axes of the slice: x: 2, y: 2, z: 4, core: 2. Of those that a mesh axis runs over, the one named last changes fastest.
Arguments:
- three_center: float32 [8192, 4, 384], P('aux', 'pair'), may hold values from -0.875 to 0.875
- occ_energy: float32 [4], P('pair'), may hold values from -1.5 to -0.3
- vir_energy: float32 [384], replicated, may hold values from 0.2 to 3
- pair_mask: int32 [4, 4], replicated, may hold values from 0 to 1, as said below
Outputs:
- gamma_aux: float32 [8192, 4, 384], P('aux', 'pair')
Inputs may be any that keep to these rules, and one draw needn't show every extreme that they name: pair_mask is symmetric and holds 1 on its diagonal.
All inputs are finite; a program needn't handle non-finite values.
Results may differ from a plain program's by a relative error of at most 0.000071.
Values sent between devices are 32-bit elements; how exact they have to be, the bound alone decides.
No kernel may reach another device: no remote copies, remote signals or barrier semaphores. Data moves between devices by JAX's collectives and lax.ppermute only.
A program may use at most 64 MiB of HBM per device.

v0:
```python
import jax
import jax.numpy as jnp
from jax import lax
from jax.sharding import PartitionSpec as P

highest = lax.Precision.HIGHEST


def from_behind(value, axis, by):
    peers = lax.axis_size(axis)
    return lax.ppermute(value, axis, [(i, (i + by) % peers) for i in range(peers)])


def contract_columns(stationary_part, moving):
    return lax.dot_general(
        stationary_part,
        moving,
        (((0,), (0,)), ((), ())),
        precision=highest,
        preferred_element_type=jnp.float32,
    )


def back_product(visitor, piece_rows):
    return lax.dot_general(
        visitor,
        piece_rows,
        (((1,), (1,)), ((), ())),
        precision=highest,
        preferred_element_type=jnp.float32,
    )


def front_product(left, right):
    return jnp.dot(left, right, precision=highest, preferred_element_type=jnp.float32)


def amplitude_block(int_slab, first_row, row_occ, col_occ, vir_energy, mask_side):
    row_total, flat_width = int_slab.shape
    virt_count = vir_energy.shape[0]
    occ_count = row_occ.shape[0]
    row_ids = first_row + jnp.arange(row_total, dtype=jnp.int32)
    occ_pick = (
        row_ids[:, None] // virt_count == jnp.arange(occ_count, dtype=jnp.int32)[None, :]
    ).astype(jnp.float32)
    vir_pick = (
        row_ids[:, None] % virt_count == jnp.arange(virt_count, dtype=jnp.int32)[None, :]
    ).astype(jnp.float32)
    row_term = jnp.dot(vir_pick, vir_energy, precision=highest) - jnp.dot(
        occ_pick, row_occ, precision=highest
    )
    col_term = vir_energy[None, :] - col_occ[:, None]
    mask_rows = jnp.dot(occ_pick, mask_side.astype(jnp.float32), precision=highest)
    denominator = row_term[:, None, None] + col_term[None, :, :]
    values = (
        mask_rows[:, :, None] * int_slab.reshape(row_total, occ_count, virt_count) / denominator
    )
    return values.reshape(row_total, flat_width)


def on_device(three_center, occ_energy, vir_energy, pair_mask):
    aux_local, occ_count, virt_count = three_center.shape
    flat_width = occ_count * virt_count
    pair_count = lax.axis_size("pair")
    aux_count = lax.axis_size("aux")
    pair_index = lax.axis_index("pair")
    slab_rows = flat_width // aux_count
    first_row = lax.axis_index("aux") * slab_rows
    resident = three_center.reshape(aux_local, flat_width)
    gamma_aux = jnp.zeros((aux_local, flat_width), jnp.float32)
    offset_total = pair_count // 2 + 1
    visitor, visitor_occ = (resident, occ_energy)
    for offset in range(offset_total):
        source = (pair_index - offset) % pair_count
        if offset > 0:
            visitor, visitor_occ = from_behind((visitor, visitor_occ), "pair", 1)
        block_mask = lax.dynamic_slice(
            pair_mask, (pair_index * occ_count, source * occ_count), (occ_count, occ_count)
        )
        block_live = jnp.any(block_mask > 0)
        stationary, moving = (resident, visitor)
        row_occ, col_occ, mask_side = (occ_energy, visitor_occ, block_mask)

        def partial_ints(
            row_start, row_total, stationary=stationary, moving=moving, block_live=block_live
        ):
            return contract_columns(stationary, moving)

        int_slab = lax.psum_scatter(
            partial_ints(jnp.int32(0), slab_rows * lax.axis_size("aux")),
            "aux",
            scatter_dimension=0,
            tiled=True,
        )
        amplitudes = amplitude_block(int_slab, first_row, row_occ, col_occ, vir_energy, mask_side)
        whole_amps = lax.all_gather(amplitudes, "aux", axis=0, tiled=True)

        def both_terms(visitor=visitor, whole_amps=whole_amps):
            return (back_product(visitor, whole_amps), front_product(resident, whole_amps))

        own_term, partner_term = both_terms()
        gamma_aux = gamma_aux + own_term
        if offset > 0 and 2 * offset < pair_count:
            gamma_aux = gamma_aux + from_behind(partner_term, "pair", pair_count - offset)
    return gamma_aux.reshape(aux_local, occ_count, virt_count)


def solution(mesh):
    in_specs = (P("aux", "pair", None), P("pair"), P(), P())
    out_specs = P("aux", "pair", None)
    return jax.shard_map(
        on_device, mesh=mesh, in_specs=in_specs, out_specs=out_specs, check_vma=False
    )
```

profile of v0, /device:TPU:0, one launch (start us, length us, event | category | flops | bytes accessed | tf_op | source)
XLA Modules:
  0.0 328.9 jit_solution(10540791383987865181)
XLA Ops:
  6.5 0.0 copy-start
  6.5 0.0 reduce-scatter.4.cloned.1.call-start
  6.5 2.8 copy.13
  9.3 0.5 collective-permute-start
  9.8 0.0 copy-done
  9.8 3.5 %fusion.8 = f32[384,384]{1,0:T(8,128)} fusion(f32[1024,1,384]{2,1,0:T(1,128)S(1)} %copy-done), kind=kOutput, calls=%fused_computation.26 | convolution fusion | flops 1811939328 | bytes 2162688 | tf_op jit(solution)/shard_map/dot_general | solution.py:15
  13.3 0.0 reduce-scatter.4.cloned.1.call-update
  13.4 0.0 reduce-scatter.6.cloned.1.call-start
  13.4 16.6 %collective-permute-done = f32[1024,384]{1,0:T(8,128)S(1)} collective-permute-done((f32[1024,384]{1,0:T(8,128)}, f32[1024,384]{1,0:T(8,128)S(1)}, u32[]{:S(2)}, u32[]{:S(2)}) %collective-permute-start) | collective-permute-done | bytes 1572896 | tf_op jit(solution)/shard_map/ppermute | solution.py:11
  30.1 0.0 collective-permute-start.3
  30.1 3.5 %fusion.6 = f32[384,384]{1,0:T(8,128)} fusion(f32[1024,384]{1,0:T(8,128)S(1)} %collective-permute-done, f32[1024,1,384]{2,1,0:T(1,128)S(1)} %copy-done), kind=kOutput, calls=%fused_computation.24 | convolution fusion | flops 1811939328 | bytes 3735552 | tf_op jit(solution)/shard_map/dot_general | solution.py:15
  33.6 0.0 reduce-scatter.6.cloned.1.call-update
  33.6 0.0 copy-start.2
  33.6 0.0 copy-start.1
  33.6 0.0 reduce-scatter.8.cloned.1.call-start
  33.7 16.3 %collective-permute-done.3 = f32[1024,384]{1,0:T(8,128)} collective-permute-done((f32[1024,384]{1,0:T(8,128)S(1)}, f32[1024,384]{1,0:T(8,128)}, u32[]{:S(2)}, u32[]{:S(2)}) %collective-permute-start.3) | collective-permute-done | bytes 1572896 | tf_op jit(solution)/shard_map/ppermute | solution.py:11
  50.0 4.9 %fusion.5 = f32[384,384]{1,0:T(8,128)} fusion(f32[1024,384]{1,0:T(8,128)} %collective-permute-done.3, f32[1024,1,384]{2,1,0:T(1,128)S(1)} %copy-done), kind=kOutput, calls=%fused_computation.23 | convolution fusion | flops 1811939328 | bytes 3735552 | tf_op jit(solution)/shard_map/dot_general | solution.py:15
  54.9 0.0 reduce-scatter.8.cloned.1.call-update
  54.9 0.1 collective-permute-start.1
  55.7 0.0 copy-done.2
  55.7 0.6 fusion.9
  58.1 0.0 copy-done.1
  58.2 0.2 fusion.1
  58.4 0.0 collective-permute-done.1
  58.4 2.4 collective-permute-start.4
  60.8 1.0 collective-permute-done.4
  61.8 1.2 broadcast_subtract_fusion
  63.0 15.7 %reduce-scatter.4.cloned.1.call-done = f32[48,384]{1,0:T(8,128)} async-done(((f32[384,384]{1,0:T(8,128)}), f32[48,384]{1,0:T(8,128)}) %reduce-scatter.4.cloned.1.call-update) | async-done | bytes 73744 | tf_op jit(solution)/shard_map/reduce_scatter | solution.py:89
  78.8 65.1 %reduce-scatter.6.cloned.1.call-done = f32[48,384]{1,0:T(8,128)} async-done(((f32[384,384]{1,0:T(8,128)}), f32[48,384]{1,0:T(8,128)}) %reduce-scatter.6.cloned.1.call-update) | async-done | bytes 73744 | tf_op jit(solution)/shard_map/reduce_scatter | solution.py:89
  143.9 65.6 %reduce-scatter.8.cloned.1.call-done = f32[48,384]{1,0:T(8,128)} async-done(((f32[384,384]{1,0:T(8,128)}), f32[48,384]{1,0:T(8,128)}) %reduce-scatter.8.cloned.1.call-update) | async-done | bytes 73744 | tf_op jit(solution)/shard_map/reduce_scatter | solution.py:89
  209.5 1.1 add_divide_fusion
  210.6 31.8 %all_gather.10 = f32[384,384]{1,0:T(8,128)S(1)} all-gather(f32[48,384]{1,0:T(8,128)S(1)} %get-tuple-element.12), channel_id=1, replica_groups=mesh['aux'=8,'pair'=4] {'aux'}, dimensions={0}, use_global_device_ids=true | all-gather | bytes 663552 | tf_op jit(solution)/shard_map/all_gather | solution.py:96
  242.4 3.9 %convolution_bitcast_fusion = f32[1024,384]{0,1:T(8,128)S(1)} fusion(f32[384,384]{1,0:T(8,128)S(1)} %all_gather.10, f32[1024,1,384]{2,1,0:T(1,128)S(1)} %copy-done), kind=kOutput, calls=%fused_computation.4 | convolution fusion | flops 1811939328 | bytes 3735552 | tf_op jit(solution)/shard_map/dot_general | solution.py:35
  246.3 0.1 collective-permute-start.2
  246.4 31.8 %all_gather.9 = f32[384,384]{1,0:T(8,128)S(1)} all-gather(f32[48,384]{1,0:T(8,128)S(1)} %get-tuple-element.13), channel_id=1, replica_groups=mesh['aux'=8,'pair'=4] {'aux'}, dimensions={0}, use_global_device_ids=true | all-gather | bytes 663552 | tf_op jit(solution)/shard_map/all_gather | solution.py:96
  278.2 31.6 %all_gather.11 = f32[384,384]{1,0:T(8,128)S(1)} all-gather(f32[48,384]{1,0:T(8,128)S(1)} %get-tuple-element.11), channel_id=1, replica_groups=mesh['aux'=8,'pair'=4] {'aux'}, dimensions={0}, use_global_device_ids=true | all-gather | bytes 663552 | tf_op jit(solution)/shard_map/all_gather | solution.py:96
  309.8 2.7 fusion.7
  312.6 2.7 fusion.10
  315.3 0.0 collective-permute-done.2
  315.3 4.3 %fusion = f32[1024,1,384]{0,2,1:T(8,128)S(1)} fusion(f32[1024,384]{0,1:T(8,128)S(1)} %collective-permute-done.2, f32[384,1024]{1,0:T(8,128)S(1)} %fusion.7, f32[384,1024]{1,0:T(8,128)S(1)} %fusion.10, f32[384,384]{1,0:T(8,128)S(1)} %all_gather.11, f32[1024,384]{1,0:T(8,128)} %collective-permute-done.3), kind=kOutput, calls=%fused_computation.2 | convolution fusion | flops 1813118976 | bytes 8454144 | tf_op jit(solution)/shard_map/dot_general | solution.py:25
  319.6 2.7 copy.5
  (4 shorter events, 0.1 us)
Async XLA Ops:
  6.5 3.3 copy-start
  6.5 72.2 %reduce-scatter.4.cloned.1.call-start = ((), (), s32[]{:S(2)}) async-start(), calls=%async_computation.3 | async-start | bytes 663552 | tf_op jit(solution)/shard_map/reduce_scatter | solution.py:89
  9.3 20.7 %collective-permute-start = (f32[1024,384]{1,0:T(8,128)}, f32[1024,384]{1,0:T(8,128)S(1)}, u32[]{:S(2)}, u32[]{:S(2)}) collective-permute-start(f32[1024,384]{1,0:T(8,128)} %bitcast.38), channel_id=1, source_target_pairs={{0,1},{1,2},{2,3},{3,0},{4,5},{5,6},{6,7},{7,4},{8,9},{9,10},{10,1... | collective-permute-start | bytes 4718600 | tf_op jit(solution)/shard_map/ppermute | solution.py:11
  13.4 130.5 %reduce-scatter.6.cloned.1.call-start = ((), (), s32[]{:S(2)}) async-start(), calls=%async_computation.4 | async-start | bytes 663552 | tf_op jit(solution)/shard_map/reduce_scatter | solution.py:89
  30.1 19.9 %collective-permute-start.3 = (f32[1024,384]{1,0:T(8,128)S(1)}, f32[1024,384]{1,0:T(8,128)}, u32[]{:S(2)}, u32[]{:S(2)}) collective-permute-start(f32[1024,384]{1,0:T(8,128)S(1)} %collective-permute-done), channel_id=1, source_target_pairs={{0,1},{1,2},{2,3},{3,0},{4,5},{5,6},{6,7},{7,4},{8,9},{9,10},{10,1... | collective-permute-start | bytes 4718600 | tf_op jit(solution)/shard_map/ppermute | solution.py:11
  33.6 22.1 %copy-start.2 = (s32[4,4]{1,0:T(4,128)S(1)}, s32[4,4]{1,0:T(4,128)}, u32[]{:S(2)}) copy-start(s32[4,4]{1,0:T(4,128)} %param.7) | copy-start | bytes 196
  33.6 24.5 %copy-start.1 = (f32[384]{0:T(512)S(1)}, f32[384]{0:T(512)}, u32[]{:S(2)}) copy-start(f32[384]{0:T(512)} %param.6) | copy-start | bytes 4612
  33.6 175.9 %reduce-scatter.8.cloned.1.call-start = ((), (), s32[]{:S(2)}) async-start(), calls=%async_computation.5 | async-start | bytes 663552 | tf_op jit(solution)/shard_map/reduce_scatter | solution.py:89
  54.9 3.5 %collective-permute-start.1 = (f32[1]{0:T(128)}, f32[1]{0:T(128)}, u32[]{:S(2)}, u32[]{:S(2)}) collective-permute-start(f32[1]{0:T(128)} %param.5), channel_id=1, source_target_pairs={{0,1},{1,2},{2,3},{3,0},{4,5},{5,6},{6,7},{7,4},{8,9},{9,10},{10,1... | collective-permute-start | bytes 20 | tf_op jit(solution)/shard_map/ppermute | solution.py:11
  58.4 3.4 %collective-permute-start.4 = (f32[1]{0:T(128)}, f32[1]{0:T(128)}, u32[]{:S(2)}, u32[]{:S(2)}) collective-permute-start(f32[1]{0:T(128)} %collective-permute-done.1), channel_id=1, source_target_pairs={{0,1},{1,2},{2,3},{3,0},{4,5},{5,6},{6,7},{7,4},{8,9},{9,10},{10,1... | collective-permute-start | bytes 20 | tf_op jit(solution)/shard_map/ppermute | solution.py:11
  246.3 68.9 %collective-permute-start.2 = (f32[1024,384]{0,1:T(8,128)S(1)}, f32[1024,384]{0,1:T(8,128)S(1)}, u32[]{:S(2)}, u32[]{:S(2)}) collective-permute-start(f32[1024,384]{0,1:T(8,128)S(1)} %convolution_bitcast_fusion), channel_id=1, source_target_pairs={{0,3},{1,0},{2,1},{3,2},{4,7},{5,4},{6,5},{7,6},{8,11},{9,8},{10,9... | collective-permute-start | bytes 4718600 | tf_op jit(solution)/shard_map/ppermute | solution.py:11
Sparse Core Ops, SparseCore 0:
  13.5 65.2 reduce-scatter.3
  82.1 61.7 reduce-scatter.5
  147.2 62.2 reduce-scatter.7
where the time goes:
time: 329 us
  waiting for transfers between devices  180 us (55%)
  blocking collectives  95.3 us (29%)
  matrix products  25.8 us (8%)
  between operations  15.7 us (5%)
  local copies, waits for them, and re-layouts  6.16 us (2%)
    reduce_scatter x3, waiting for transfers between devices, on_device(): lax.psum_scatter(partial_ints(jnp.int32(0), slab_rows * lax.axis_size('au...  146 us
    all_gather x3, blocking collectives, on_device(): whole_amps = lax.all_gather(amplitudes, 'aux', axis=0, tiled=True)  95.3 us
    ppermute x5, waiting for transfers between devices, from_behind(): lax.ppermute(value, axis, [(i, (i + by) % peers) for i in range(peers)])  34 us
    dot_general x3, matrix products, contract_columns(): lax.dot_general(stationary_part, moving, (((0,), (0,)), ((), ())), precis...  11.9 us
    dot_general x3, matrix products, back_product(): lax.dot_general(visitor, piece_rows, (((1,), (1,)), ((), ())), precision=...  9.75 us
  transfers between devices with their start and end apart: 8, of which 6 were waited for; matrix products, arithmetic and copies ran while one was open for 6% of the time, Pallas kernels for 0%

commit v1 on v0

v1 whole, which is shorter than its diff:
```python
import jax
import jax.numpy as jnp
from jax import lax
from jax.sharding import PartitionSpec as P

AXES = ("aux", "pair")
precision = lax.Precision.HIGH


def across(value, aux_flip, pair_flip):
    aux_count, pair_count = lax.axis_size("aux"), lax.axis_size("pair")
    moves = [
        (a * pair_count + p, (a ^ aux_flip) * pair_count + (p ^ pair_flip))
        for a in range(aux_count)
        for p in range(pair_count)
    ]
    return lax.ppermute(value, AXES, moves)


def pick(pieces, index):
    return lax.dynamic_index_in_dim(pieces, index, 0, keepdims=False)


def tn(left, right):
    return lax.dot_general(
        left, right, (((0,), (0,)), ((), ())), precision=precision,
        preferred_element_type=jnp.float32)


def nt(left, right):
    return lax.dot_general(
        left, right, (((1,), (1,)), ((), ())), precision=precision,
        preferred_element_type=jnp.float32)


def nn(left, right):
    return jnp.dot(left, right, precision=precision, preferred_element_type=jnp.float32)


def scatter_sum(value, flips, index):
    members = len(flips)
    pieces = value.reshape((members, value.shape[0] // members) + value.shape[1:])
    total = pick(pieces, index)
    for step in range(1, members):
        total = total + across(pick(pieces, index ^ step), *flips[step])
    return total


def gather(piece, flips, index):
    members = len(flips)
    whole = jnp.zeros((members,) + piece.shape, piece.dtype)
    whole = lax.dynamic_update_index_in_dim(whole, piece, index, 0)
    for step in range(1, members):
        whole = lax.dynamic_update_index_in_dim(
            whole, across(piece, *flips[step]), index ^ step, 0)
    return whole.reshape((members * piece.shape[0],) + piece.shape[1:])


def aux_groups(aux_count):
    bits = aux_count.bit_length() - 1
    low, groups = 1, []
    while low < bits:
        width = min(2, bits - low)
        groups.append((low, width))
        low += width
    return groups


def on_device(three_center, occ_energy, vir_energy, pair_mask):
    rows, occ_count, virt = three_center.shape
    aux_count = lax.axis_size("aux")
    aux, pair = lax.axis_index("aux"), lax.axis_index("pair")
    side, lane = pair // 2, pair % 2
    half = rows // 2
    own = three_center.reshape(rows, virt)
    pieces = own.reshape(2, half, virt)
    occ_side = jnp.stack([occ_energy[0], across(occ_energy, 0, 1)[0]])
    occ_side = jnp.where(lane == 0, occ_side, occ_side[::-1])
    occ_other = across(occ_side, 0, 2)
    occ_low = jnp.where(side == 0, occ_side, occ_other)
    occ_high = jnp.where(side == 0, occ_other, occ_side)
    mask = pair_mask.astype(jnp.float32)

    facing_near = across(pick(pieces, side ^ 1), 0, 2)
    twin = across(own, 0, 1)
    facing_far = across(pick(pieces, side), 0, 2)

    z_groups = aux_groups(aux_count)

    def z_scatter(value):
        start = jnp.int32(0)
        for low, width in z_groups:
            members = 1 << width
            index = (aux >> low) & (members - 1)
            value = scatter_sum(value, [(s << low, 0) for s in range(members)], index)
            start = start + index * value.shape[0]
        return value, start

    def z_gather(value):
        for low, width in reversed(z_groups):
            members = 1 << width
            index = (aux >> low) & (members - 1)
            value = gather(value, [(s << low, 0) for s in range(members)], index)
        return value

    first = jnp.where(lane == 0, own, twin)
    second = jnp.where(lane == 0, twin, own)
    near = virt // 2
    left = lax.dynamic_slice_in_dim(first, lane * near, near, 1)
    side_ints = jnp.concatenate([tn(own, own), tn(left, second)], 0)
    x_flips = [(0, 0), (1, 0)]
    x_index = aux & 1
    part = scatter_sum(side_ints, x_flips, x_index)
    start = x_index * part.shape[0]
    part, more = z_scatter(part)
    start = start + more
    row = start + jnp.arange(part.shape[0])
    in_own = row < virt
    a_index = jnp.where(in_own, row, row - virt + lane * near)
    occ_i = jnp.where(in_own, pick(occ_side, lane), occ_side[0])
    occ_j = jnp.where(in_own, pick(occ_side, lane), occ_side[1])
    weight = jnp.where(
        in_own, mask[pair, pair], mask[2 * side, 2 * side + 1])
    row_term = jnp.take(vir_energy, a_index) - occ_i - occ_j
    part = weight[:, None] * part / (row_term[:, None] + vir_energy[None, :])
    side_amps = gather(z_gather(part), x_flips, x_index)
    own_amps = side_amps[:virt]
    mixed = side_amps[virt:]
    mixed_twin = across(mixed, 0, 1)
    mixed_amps = jnp.concatenate(
        [jnp.where(lane == 0, mixed, mixed_twin), jnp.where(lane == 0, mixed_twin, mixed)], 0)

    here = pick(pieces, side)
    twin_here = pick(twin.reshape(2, half, virt), side)
    facing_twin = across(facing_near, 0, 1)
    low = jnp.where(side == 0, here, facing_near)
    high = jnp.where(side == 0, facing_near, here)
    high_twin = jnp.where(side == 0, facing_twin, twin_here)
    high_first = jnp.where(lane == 0, high, high_twin)
    high_second = jnp.where(lane == 0, high_twin, high)
    cross_ints = jnp.concatenate([tn(low, high_first), tn(low, high_second)], 0)
    q_flips = [(0, 0), (1, 0), (0, 2), (1, 2)]
    q_index = (aux & 1) + 2 * side
    part = scatter_sum(cross_ints, q_flips, q_index)
    start = q_index * part.shape[0]
    part, more = z_scatter(part)
    start = start + more
    row = start + jnp.arange(part.shape[0])
    block = row // virt
    a_index = row % virt
    weight = jnp.where(block == 0, mask[lane, 2], mask[lane, 3])
    row_term = jnp.take(vir_energy, a_index) - pick(occ_low, lane) - jnp.where(
        block == 0, occ_high[0], occ_high[1])
    part = weight[:, None] * part / (row_term[:, None] + vir_energy[None, :])
    cross_amps = gather(z_gather(part), q_flips, q_index)

    cross_blocks = cross_amps.reshape(2, virt, virt)
    swapped = across(pick(cross_blocks, lane ^ 1), 0, 1)
    kept = pick(cross_blocks, lane)
    facing_far_twin = across(facing_far, 0, 1)
    zero_near = jnp.where(side == 0, facing_near, facing_far)
    zero_far = jnp.where(side == 0, facing_far, facing_near)
    facing = jnp.concatenate([zero_near, zero_far], 0)
    twin_near = jnp.where(side == 0, facing_twin, facing_far_twin)
    twin_far = jnp.where(side == 0, facing_far_twin, facing_twin)
    facing_t = jnp.concatenate([twin_near, twin_far], 0)
    f_first = jnp.where(lane == 0, facing, facing_t)
    f_second = jnp.where(lane == 0, facing_t, facing)
    low_amps = jnp.where(lane == 0, kept, swapped)
    high_amps = jnp.where(lane == 0, swapped, kept)
    m0 = jnp.where(side == 0, cross_blocks[0], low_amps.T)
    m1 = jnp.where(side == 0, cross_blocks[1], high_amps.T)
    mixed_use = jnp.where(lane == 0, mixed_amps, mixed_amps.T)
    gamma = nt(own, own_amps) + nt(twin, mixed_use) + nt(f_first, m0) + nt(f_second, m1)
    return gamma.reshape(rows, occ_count, virt)


def solution(mesh):
    in_specs = (P("aux", "pair", None), P("pair"), P(), P())
    out_specs = P("aux", "pair", None)
    return jax.shard_map(
        on_device, mesh=mesh, in_specs=in_specs, out_specs=out_specs, check_vma=False
    )
```

time: 329 us -> 149 us (0.45)
  waiting for transfers between devices: 180 us -> 43 us
  blocking collectives: 95.3 us -> 0 us
  starting transfers between devices: 3.14 us -> 34.5 us
  local copies, waits for them, and re-layouts: 6.16 us -> 27.6 us
  between operations: 15.7 us -> 1.3 us
  other arithmetic: 2.33 us -> 14.3 us
    reduce_scatter x3 -> x0, waiting for transfers between devices: 146 us -> none  [on_device(): lax.psum_scatter(partial_ints(jnp.int32(0), slab_rows * lax.axis_size('au...]
    all_gather x3 -> x0, blocking collectives: 95.3 us -> none  [on_device(): whole_amps = lax.all_gather(amplitudes, 'aux', axis=0, tiled=True)]
    ppermute x5 -> x29, starting transfers between devices: 3.05 us -> 34.5 us  [across(): return lax.ppermute(value, AXES, moves)]
    ppermute x5 -> x29, waiting for transfers between devices: 34 us -> 43 us  [across(): return lax.ppermute(value, AXES, moves)]
    select_n x1 -> x9, other arithmetic: 0.01 us -> 7.97 us  [the longest x1 2.43 us: on_device(): zero_near = jnp.where(side == 0, facing_near, facing_far)]
    squeeze x0 -> x8, local copies, waits for them, and re-layouts: none -> 5.62 us  [the longest x1 2.29 us: on_device(): m1 = jnp.where(side == 0, cross_blocks[1], high_amps.T)]
    dynamic_update_slice x0 -> x12, local copies, waits for them, and re-layouts: none -> 4.95 us  [the longest x10 3.87 us: gather(): lax.dynamic_update_index_in_dim(whole, across(piece, *flips[step]), index...]
  transfers between devices with their start and end apart: 8 -> 29, of which waited for: 6 -> 13; matrix products, arithmetic and copies ran while one was open for 6% -> 33% of each run, Pallas kernels for 0% -> 0%
where the time goes in v1:
time: 149 us; the launch traced here: 146 us
  waiting for transfers between devices  43 us (29%)
  starting transfers between devices  34.5 us (23%)
  local copies, waits for them, and re-layouts  27.6 us (19%)
  matrix products  25.5 us (17%)
  other arithmetic  14.3 us (10%)
    ppermute x29, waiting for transfers between devices, across(): return lax.ppermute(value, AXES, moves)  43 us
    ppermute x29, starting transfers between devices, across(): return lax.ppermute(value, AXES, moves)  34.5 us
    dot_general x4, matrix products, nt(): lax.dot_general(left, right, (((1,), (1,)), ((), ())), precision=precisio...  14.3 us
    dot_general x4, matrix products, tn(): lax.dot_general(left, right, (((0,), (0,)), ((), ())), precision=precisio...  11.2 us
    reshape x1, local copies, waits for them, and re-layouts, on_device(): return gamma.reshape(rows, occ_count, virt)  4.81 us
    dynamic_update_slice x10, local copies, waits for them, and re-layouts, gather(): lax.dynamic_update_index_in_dim(whole, across(piece, *flips[step]), index...  3.87 us
  transfers between devices with their start and end apart: 29, of which 13 were waited for; matrix products, arithmetic and copies ran while one was open for 33% of the time, Pallas kernels for 0%

profile of v1, /device:TPU:0, one launch (start us, length us, event | category | flops | bytes accessed | tf_op | source)
XLA Modules:
  0.0 146.3 jit_solution(9872888298648225035)
XLA Ops:
  0.0 1.5 %copy.47 = f32[1024,1,384]{2,0,1:T(8,128)S(1)} copy(f32[1024,1,384]{2,1,0:T(1,128)} %param.4) | data formatting | bytes 3145728
  2.2 1.2 dynamic-slice_bitcast_fusion.1
  3.4 2.9 %collective-permute-start.11 = (f32[512,384]{1,0:T(8,128)}, f32[512,384]{1,0:T(8,128)S(1)}, u32[]{:S(2)}, u32[]{:S(2)}) collective-permute-start(f32[512,384]{1,0:T(8,128)} %get-tuple-element.15), channel_id=1, source_target_pairs={{0,2},{1,3},{2,0},{3,1},{4,6},{5,7},{6,4},{7,5},{8,10},{9,11},{10,... | collective-permute-start | bytes 2359304 | tf_op jit(solution)/shard_map/ppermute | solution.py:17
  6.4 3.3 %fusion.54 = f32[384,384]{1,0:T(8,128)S(1)} fusion(f32[1024,1,384]{2,1,0:T(1,128)} %param.4), kind=kOutput, calls=%fused_computation.131 | convolution fusion | flops 905969664 | bytes 2162688 | tf_op jit(solution)/shard_map/dot_general | solution.py:25
  9.9 0.7 fusion.61
  10.5 1.3 compare_select_fusion.8
  11.9 1.3 compare_select_fusion.6
  13.9 1.4 gather_fusion
  15.4 0.8 gather_fusion.1
  17.6 2.0 %collective-permute-start.21 = (f32[2]{0:T(128)S(1)}, f32[2]{0:T(128)S(1)}, u32[]{:S(2)}, u32[]{:S(2)}) collective-permute-start(f32[2]{0:T(128)S(1)} %broadcast_select_fusion.14), channel_id=1, source_target_pairs={{0,2},{1,3},{2,0},{3,1},{4,6},{5,7},{6,4},{7,5},{8,10},{9,11},{10,... | collective-permute-start | bytes 32 | tf_op jit(solution)/shard_map/ppermute | solution.py:17
  19.5 0.6 fusion.62
  20.2 1.9 %select_subtract_fusion = f32[72]{0:T(128)S(1)} fusion(f32[72]{0:T(128)S(1)} %gather_fusion, f32[]{:T(128)} %bitcast.13, f32[]{:T(128)} %bitcast.12, f32[]{:T(128)} %bitcast.11, s32[]{:T(128)S(6)} %mul.41, s32[]{:T(128)S(6)} %add.335), kind=kLoop, calls=%fused_computation.121 | loop fusion | flops 1152 | bytes 596 | tf_op jit(solution)/shard_map/sub | solution.py:124
  22.0 2.9 %collective-permute-done.11 = f32[512,384]{1,0:T(8,128)S(1)} collective-permute-done((f32[512,384]{1,0:T(8,128)}, f32[512,384]{1,0:T(8,128)S(1)}, u32[]{:S(2)}, u32[]{:S(2)}) %collective-permute-start.11) | collective-permute-done | bytes 786464 | tf_op jit(solution)/shard_map/ppermute | solution.py:17
  24.9 16.4 %collective-permute-done.21 = f32[2]{0:T(128)S(1)} collective-permute-done((f32[2]{0:T(128)S(1)}, f32[2]{0:T(128)S(1)}, u32[]{:S(2)}, u32[]{:S(2)}) %collective-permute-start.21) | collective-permute-done | bytes 40 | tf_op jit(solution)/shard_map/ppermute | solution.py:17
  41.3 0.6 dynamic_slice.110
  42.5 1.9 %fusion.46 = f32[48]{0:T(128)S(1)} fusion(f32[48]{0:T(128)S(1)} %gather_fusion.1, f32[]{:T(128)} %bitcast.43, f32[]{:T(128)} %bitcast.42, f32[]{:T(128)} %bitcast.41, s32[]{:T(128)S(6)} %add.371), kind=kLoop, calls=%fused_computation.115 | loop fusion | flops 1152 | bytes 400 | tf_op jit(solution)/shard_map/sub | solution.py:152
  44.5 2.4 %broadcast_select_fusion.5 = (f32[512,384]{1,0:T(8,128)}, f32[512,384]{1,0:T(8,128)}) fusion(f32[512,384]{1,0:T(8,128)S(1)} %collective-permute-done.11, f32[512,384]{1,0:T(8,128)} %collective-permute-done.12, pred[]{:T(512)S(6)} %eq.18), kind=kLoop, calls=%fused_computation.51 | loop fusion | flops 393216 | bytes 3145729 | tf_op jit(solution)/shard_map/jit(_where)/select_n | solution.py:161
  46.9 2.1 %fusion.13 = f32[384,384]{1,0:T(8,128)S(1)} fusion(pred[]{:T(512)S(6)} %eq.17, f32[512,384]{1,0:T(8,128)S(1)} %collective-permute-done.11, pred[]{:T(512)S(6)} %eq.18, f32[512,384]{1,0:T(8,128)S(1)} %collective-permute-done.13, f32[2,512,384]{2,1,0:T(8,128)} %bitcast.28, s32[]{:T(128)S(6)} %select_n.394, f32[2,512,384]{2,1,0:T(8,128)S(1)} %bitcast.166), kind=kOutput, calls=%fused_computation.20 | convolution fusion | flops 453771264 | bytes 5310976 | tf_op jit(solution)/shard_map/dot_general | solution.py:25
  49.0 2.0 %fusion.11 = f32[384,384]{1,0:T(8,128)S(1)} fusion(pred[]{:T(512)S(6)} %eq.17, f32[512,384]{1,0:T(8,128)S(1)} %collective-permute-done.11, pred[]{:T(512)S(6)} %eq.18, f32[512,384]{1,0:T(8,128)S(1)} %collective-permute-done.13, f32[2,512,384]{2,1,0:T(8,128)} %bitcast.28, s32[]{:T(128)S(6)} %select_n.394, f32[2,512,384]{2,1,0:T(8,128)S(1)} %bitcast.167), kind=kOutput, calls=%fused_computation.18 | convolution fusion | flops 453771264 | bytes 5310976 | tf_op jit(solution)/shard_map/dot_general | solution.py:25
  51.2 1.8 %collective-permute-start.15 = (f32[192,384]{1,0:T(8,128)S(1)}, f32[192,384]{1,0:T(8,128)S(1)}, u32[]{:S(2)}, u32[]{:S(2)}) collective-permute-start(f32[192,384]{1,0:T(8,128)S(1)} %get-tuple-element.21), channel_id=1, source_target_pairs={{0,4},{1,5},{2,6},{3,7},{4,0},{5,1},{6,2},{7,3},{8,12},{9,13},{10,... | collective-permute-start | bytes 884744 | tf_op jit(solution)/shard_map/ppermute | solution.py:17
  53.0 1.5 %collective-permute-start.16 = (f32[192,384]{1,0:T(8,128)S(1)}, f32[192,384]{1,0:T(8,128)S(1)}, u32[]{:S(2)}, u32[]{:S(2)}) collective-permute-start(f32[192,384]{1,0:T(8,128)S(1)} %get-tuple-element.23), channel_id=1, source_target_pairs={{0,2},{1,3},{2,0},{3,1},{4,6},{5,7},{6,4},{7,5},{8,10},{9,11},{10,... | collective-permute-start | bytes 884744 | tf_op jit(solution)/shard_map/ppermute | solution.py:17
  54.7 3.8 %fusion.6 = f32[192,384]{1,0:T(8,128)S(1)} fusion(f32[1024,384]{1,0:T(8,128)} %collective-permute-done, f32[1024,384]{1,0:T(8,128)S(1)} %bitcast.168, s32[]{:T(128)S(6)} %select_n.369, pred[]{:T(512)S(6)} %eq.17), kind=kOutput, calls=%fused_computation.11 | convolution fusion | flops 453574656 | bytes 5539328 | tf_op jit(solution)/shard_map/dot_general | solution.py:25
  58.6 1.8 %collective-permute-start.1 = (f32[288,384]{1,0:T(8,128)S(1)}, f32[288,384]{1,0:T(8,128)S(1)}, u32[]{:S(2)}, u32[]{:S(2)}) collective-permute-start(f32[288,384]{1,0:T(8,128)S(1)} %dynamic-slice_bitcast_fusion.3), channel_id=1, source_target_pairs={{0,4},{1,5},{2,6},{3,7},{4,0},{5,1},{6,2},{7,3},{8,12},{9,13},{10,... | collective-permute-start | bytes 1327112 | tf_op jit(solution)/shard_map/ppermute | solution.py:17
  60.4 0.7 collective-permute-done.15
  61.1 7.0 %collective-permute-done.16 = f32[192,384]{1,0:T(8,128)S(1)} collective-permute-done((f32[192,384]{1,0:T(8,128)S(1)}, f32[192,384]{1,0:T(8,128)S(1)}, u32[]{:S(2)}, u32[]{:S(2)}) %collective-permute-start.16) | collective-permute-done | bytes 294944 | tf_op jit(solution)/shard_map/ppermute | solution.py:17
  68.8 1.6 %collective-permute-start.18 = (f32[48,384]{1,0:T(8,128)S(1)}, f32[48,384]{1,0:T(8,128)S(1)}, u32[]{:S(2)}, u32[]{:S(2)}) collective-permute-start(f32[48,384]{1,0:T(8,128)S(1)} %get-tuple-element.27), channel_id=1, source_target_pairs={{0,8},{1,9},{2,10},{3,11},{4,12},{5,13},{6,14},{7,15},{8,0},{9,1},... | collective-permute-start | bytes 221192 | tf_op jit(solution)/shard_map/ppermute | solution.py:17
  70.4 2.6 %collective-permute-start.19 = (f32[48,384]{1,0:T(8,128)S(1)}, f32[48,384]{1,0:T(8,128)S(1)}, u32[]{:S(2)}, u32[]{:S(2)}) collective-permute-start(f32[48,384]{1,0:T(8,128)S(1)} %get-tuple-element.29), channel_id=1, source_target_pairs={{0,16},{1,17},{2,18},{3,19},{4,20},{5,21},{6,22},{7,23},{8,24},{9,... | collective-permute-start | bytes 221192 | tf_op jit(solution)/shard_map/ppermute | solution.py:17
  73.2 1.3 broadcast_select_fusion.3
  74.5 3.0 %collective-permute-done.19 = f32[48,384]{1,0:T(8,128)S(1)} collective-permute-done((f32[48,384]{1,0:T(8,128)S(1)}, f32[48,384]{1,0:T(8,128)S(1)}, u32[]{:S(2)}, u32[]{:S(2)}) %collective-permute-start.19) | collective-permute-done | bytes 73760 | tf_op jit(solution)/shard_map/ppermute | solution.py:17
  77.5 1.6 %collective-permute-done.20 = f32[48,384]{1,0:T(8,128)S(1)} collective-permute-done((f32[48,384]{1,0:T(8,128)S(1)}, f32[48,384]{1,0:T(8,128)S(1)}, u32[]{:S(2)}, u32[]{:S(2)}) %collective-permute-start.20) | collective-permute-done | bytes 73760 | tf_op jit(solution)/shard_map/ppermute | solution.py:17
  79.3 2.2 %collective-permute-start.23 = (f32[48,384]{1,0:T(8,128)S(1)}, f32[48,384]{1,0:T(8,128)S(1)}, u32[]{:S(2)}, u32[]{:S(2)}) collective-permute-start(f32[48,384]{1,0:T(8,128)S(1)} %get-tuple-element.8), channel_id=1, source_target_pairs={{0,16},{1,17},{2,18},{3,19},{4,20},{5,21},{6,22},{7,23},{8,24},{9,... | collective-permute-start | bytes 221192 | tf_op jit(solution)/shard_map/ppermute | solution.py:17
  81.5 2.2 %collective-permute-start.24 = (f32[48,384]{1,0:T(8,128)S(1)}, f32[48,384]{1,0:T(8,128)S(1)}, u32[]{:S(2)}, u32[]{:S(2)}) collective-permute-start(f32[48,384]{1,0:T(8,128)S(1)} %get-tuple-element.8), channel_id=1, source_target_pairs={{0,24},{1,25},{2,26},{3,27},{4,28},{5,29},{6,30},{7,31},{8,16},{9,... | collective-permute-start | bytes 221192 | tf_op jit(solution)/shard_map/ppermute | solution.py:17
  83.9 2.2 %collective-permute-start.3 = (f32[72,384]{1,0:T(8,128)S(1)}, f32[72,384]{1,0:T(8,128)S(1)}, u32[]{:S(2)}, u32[]{:S(2)}) collective-permute-start(f32[72,384]{1,0:T(8,128)S(1)} %get-tuple-element.26), channel_id=1, source_target_pairs={{0,16},{1,17},{2,18},{3,19},{4,20},{5,21},{6,22},{7,23},{8,24},{9,... | collective-permute-start | bytes 331784 | tf_op jit(solution)/shard_map/ppermute | solution.py:17
  86.1 2.2 %collective-permute-start.4 = (f32[72,384]{1,0:T(8,128)S(1)}, f32[72,384]{1,0:T(8,128)S(1)}, u32[]{:S(2)}, u32[]{:S(2)}) collective-permute-start(f32[72,384]{1,0:T(8,128)S(1)} %get-tuple-element.25), channel_id=1, source_target_pairs={{0,24},{1,25},{2,26},{3,27},{4,28},{5,29},{6,30},{7,31},{8,16},{9,... | collective-permute-start | bytes 331784 | tf_op jit(solution)/shard_map/ppermute | solution.py:17
  88.6 1.5 %collective-permute-start.25 = (f32[192,384]{1,0:T(8,128)S(1)}, f32[192,384]{1,0:T(8,128)S(1)}, u32[]{:S(2)}, u32[]{:S(2)}) collective-permute-start(f32[192,384]{1,0:T(8,128)S(1)} %bitcast.183), channel_id=1, source_target_pairs={{0,4},{1,5},{2,6},{3,7},{4,0},{5,1},{6,2},{7,3},{8,12},{9,13},{10,... | collective-permute-start | bytes 884744 | tf_op jit(solution)/shard_map/ppermute | solution.py:17
  90.7 1.5 %collective-permute-start.27 = (f32[192,384]{1,0:T(8,128)S(1)}, f32[192,384]{1,0:T(8,128)S(1)}, u32[]{:S(2)}, u32[]{:S(2)}) collective-permute-start(f32[192,384]{1,0:T(8,128)S(1)} %bitcast.185), channel_id=1, source_target_pairs={{0,6},{1,7},{2,4},{3,5},{4,2},{5,3},{6,0},{7,1},{8,14},{9,15},{10,... | collective-permute-start | bytes 884744 | tf_op jit(solution)/shard_map/ppermute | solution.py:17
  92.2 4.0 %collective-permute-done.3 = f32[72,384]{1,0:T(8,128)S(1)} collective-permute-done((f32[72,384]{1,0:T(8,128)S(1)}, f32[72,384]{1,0:T(8,128)S(1)}, u32[]{:S(2)}, u32[]{:S(2)}) %collective-permute-start.3) | collective-permute-done | bytes 110624 | tf_op jit(solution)/shard_map/ppermute | solution.py:17
  96.2 0.8 broadcast_in_dim.109
  97.1 0.7 bitcast_dynamic-update-slice_fusion.9
  97.8 2.0 %collective-permute-start.6 = (f32[72,384]{1,0:T(8,128)S(1)}, f32[72,384]{1,0:T(8,128)S(1)}, u32[]{:S(2)}, u32[]{:S(2)}) collective-permute-start(f32[72,384]{1,0:T(8,128)S(1)} %get-tuple-element.6), channel_id=1, source_target_pairs={{0,8},{1,9},{2,10},{3,11},{4,12},{5,13},{6,14},{7,15},{8,0},{9,1},... | collective-permute-start | bytes 331784 | tf_op jit(solution)/shard_map/ppermute | solution.py:17
  100.0 1.0 collective-permute-start.7
  101.0 2.7 %collective-permute-done.6 = f32[72,384]{1,0:T(8,128)S(1)} collective-permute-done((f32[72,384]{1,0:T(8,128)S(1)}, f32[72,384]{1,0:T(8,128)S(1)}, u32[]{:S(2)}, u32[]{:S(2)}) %collective-permute-start.6) | collective-permute-done | bytes 110624 | tf_op jit(solution)/shard_map/ppermute | solution.py:17
  103.7 1.8 %collective-permute-start.8 = (f32[72,384]{1,0:T(8,128)S(1)}, f32[72,384]{1,0:T(8,128)S(1)}, u32[]{:S(2)}, u32[]{:S(2)}) collective-permute-start(f32[72,384]{1,0:T(8,128)S(1)} %get-tuple-element.6), channel_id=1, source_target_pairs={{0,24},{1,25},{2,26},{3,27},{4,28},{5,29},{6,30},{7,31},{8,16},{9,... | collective-permute-start | bytes 331784 | tf_op jit(solution)/shard_map/ppermute | solution.py:17
  105.5 0.7 bitcast_dynamic-update-slice_fusion.8
  106.1 3.0 %collective-permute-done.7 = f32[72,384]{1,0:T(8,128)S(1)} collective-permute-done((f32[72,384]{1,0:T(8,128)S(1)}, f32[72,384]{1,0:T(8,128)S(1)}, u32[]{:S(2)}, u32[]{:S(2)}) %collective-permute-start.7) | collective-permute-done | bytes 110624 | tf_op jit(solution)/shard_map/ppermute | solution.py:17
  109.1 0.6 bitcast_dynamic-update-slice_fusion.7
  110.3 0.7 bitcast_dynamic-update-slice_fusion.6
  111.0 1.4 collective-permute-start.9
  112.5 1.1 bitcast_dynamic-update-slice_fusion.1
  113.7 0.8 copy-done.11
  114.4 0.9 dynamic-slice_bitcast_fusion.2
  115.3 0.9 fusion.60
  116.2 1.0 copy.28
  117.2 2.3 %copy.30 = f32[384,384]{0,1:T(8,128)} copy(f32[384,384]{1,0:T(8,128)} %bitcast.179) | data formatting | bytes 1179648 | tf_op jit(solution)/shard_map/squeeze | solution.py:172
  119.8 1.8 %bitcast_dynamic-update-slice_fusion = f32[2,288,384]{2,1,0:T(8,128)} fusion(f32[2,288,384]{2,1,0:T(8,128)} %copy-done.11, s32[]{:T(128)S(6)} %select_n.372, f32[288,384]{1,0:T(8,128)} %collective-permute-done.9), kind=kLoop, calls=%fused_computation.40 | loop fusion | bytes 884740 | tf_op jit(solution)/shard_map/jit(dynamic_update_index_in_dim)/dynamic_update_slice | solution.py:54
  121.6 1.0 slice.39
  122.9 3.9 %fusion.18 = f32[384,1024]{1,0:T(8,128)} fusion(f32[576,384]{1,0:T(8,128)} %bitcast.173, f32[1024,1,384]{2,1,0:T(1,128)S(1)} %copy-done.1), kind=kOutput, calls=%fused_computation.27 | convolution fusion | flops 905969664 | bytes 3735552 | tf_op jit(solution)/shard_map/dot_general | solution.py:31
  126.9 2.7 %fusion.4 = f32[1024,384]{0,1:T(8,128)} fusion(f32[512,384]{1,0:T(8,128)S(1)} %copy-done.8, f32[512,384]{1,0:T(8,128)S(1)} %copy-done.6, f32[512,384]{1,0:T(8,128)S(1)} %copy-done.4, f32[512,384]{1,0:T(8,128)S(1)} %copy-done.2, pred[]{:T(512)S(6)} %eq.17, f32[384,384]{0,1:T(8,128)S(1)} %copy-done.13, f32[384,384]{1,0:T(8,128)} %collective-permute-done.28, ...), kind=kOutput, calls=%fused_computation.9 | convolution fusion | flops 907444224 | bytes 6490112 | tf_op jit(solution)/shard_map/dot_general | solution.py:31
  129.5 1.0 broadcast_select_fusion.11
  130.5 0.9 pad_maximum_fusion.8
  131.4 2.2 %copy.27 = f32[384,384]{0,1:T(8,128)} copy(f32[384,384]{1,0:T(8,128)} %pad_maximum_fusion.8) | data formatting | bytes 1179648 | tf_op jit(solution)/shard_map/concatenate | solution.py:130
  133.7 3.2 %fusion.20 = f32[384,1024]{1,0:T(8,128)S(1)} fusion(f32[1024,384]{1,0:T(8,128)} %collective-permute-done, f32[384,384]{0,1:T(8,128)} %copy.27, pred[]{:T(512)S(6)} %eq.17, f32[192,384]{1,0:T(8,128)S(1)} %get-tuple-element.20, f32[192,384]{1,0:T(8,128)S(1)} %get-tuple-element.19), kind=kOutput, calls=%fused_computation.35 | convolution fusion | flops 906264576 | bytes 4325377 | tf_op jit(solution)/shard_map/dot_general | solution.py:31
  136.9 4.6 %fusion.1 = f32[1024,1,384]{0,2,1:T(8,128)} fusion(f32[1024,384]{0,1:T(8,128)} %fusion.4, f32[384,1024]{1,0:T(8,128)S(1)} %copy-done.10, f32[384,1024]{1,0:T(8,128)S(1)} %fusion.20, f32[512,384]{1,0:T(8,128)S(1)} %copy-done.9, f32[512,384]{1,0:T(8,128)S(1)} %copy-done.7, f32[512,384]{1,0:T(8,128)S(1)} %copy-done.5, f32[512,384]{1,0:T(8,128)S(1)} %copy-done.3, ...), kind=kOutput, calls=%fused_computation.6 | convolution fusion | flops 908623872 | bytes 11208704 | tf_op jit(solution)/shard_map/dot_general | solution.py:31
  141.5 4.8 %copy.32 = f32[1024,1,384]{2,1,0:T(1,128)} copy(f32[1024,1,384]{0,2,1:T(8,128)} %fusion.1) | data formatting | bytes 3145728 | tf_op jit(solution)/shard_map/reshape | solution.py:175
  (90 shorter events, 6.7 us)
Async XLA Ops:
  1.5 45.4 %collective-permute-start = (f32[1024,384]{1,0:T(8,128)S(1)}, f32[1024,384]{1,0:T(8,128)}, u32[]{:S(2)}, u32[]{:S(2)}) collective-permute-start(f32[1024,384]{1,0:T(8,128)S(1)} %bitcast.164), channel_id=1, source_target_pairs={{0,1},{1,0},{2,3},{3,2},{4,5},{5,4},{6,7},{7,6},{8,9},{9,8},{10,11... | collective-permute-start | bytes 4718600 | tf_op jit(solution)/shard_map/ppermute | solution.py:17
  2.1 14.1 %collective-permute-start.5 = (f32[1]{0:T(128)}, f32[1]{0:T(128)}, u32[]{:S(2)}, u32[]{:S(2)}) collective-permute-start(f32[1]{0:T(128)} %param.5), channel_id=1, source_target_pairs={{0,1},{1,0},{2,3},{3,2},{4,5},{5,4},{6,7},{7,6},{8,9},{9,8},{10,11... | collective-permute-start | bytes 20 | tf_op jit(solution)/shard_map/ppermute | solution.py:17
  3.4 6.3 %copy-start.14 = (s32[4,4]{1,0:T(4,128)S(1)}, s32[4,4]{1,0:T(4,128)}, u32[]{:S(2)}) copy-start(s32[4,4]{1,0:T(4,128)} %param.7) | copy-start | bytes 196
  3.4 10.5 %copy-start = (f32[384]{0:T(512)S(1)}, f32[384]{0:T(512)}, u32[]{:S(2)}) copy-start(f32[384]{0:T(512)} %param.6) | copy-start | bytes 4612
  3.4 21.5 %collective-permute-start.11 = (f32[512,384]{1,0:T(8,128)}, f32[512,384]{1,0:T(8,128)S(1)}, u32[]{:S(2)}, u32[]{:S(2)}) collective-permute-start(f32[512,384]{1,0:T(8,128)} %get-tuple-element.15), channel_id=1, source_target_pairs={{0,2},{1,3},{2,0},{3,1},{4,6},{5,7},{6,4},{7,5},{8,10},{9,11},{10,... | collective-permute-start | bytes 2359304 | tf_op jit(solution)/shard_map/ppermute | solution.py:17
  6.3 38.1 %collective-permute-start.12 = (f32[512,384]{1,0:T(8,128)}, f32[512,384]{1,0:T(8,128)}, u32[]{:S(2)}, u32[]{:S(2)}) collective-permute-start(f32[512,384]{1,0:T(8,128)} %get-tuple-element.16), channel_id=1, source_target_pairs={{0,2},{1,3},{2,0},{3,1},{4,6},{5,7},{6,4},{7,5},{8,10},{9,11},{10,... | collective-permute-start | bytes 2359304 | tf_op jit(solution)/shard_map/ppermute | solution.py:17
  17.6 23.7 %collective-permute-start.21 = (f32[2]{0:T(128)S(1)}, f32[2]{0:T(128)S(1)}, u32[]{:S(2)}, u32[]{:S(2)}) collective-permute-start(f32[2]{0:T(128)S(1)} %broadcast_select_fusion.14), channel_id=1, source_target_pairs={{0,2},{1,3},{2,0},{3,1},{4,6},{5,7},{6,4},{7,5},{8,10},{9,11},{10,... | collective-permute-start | bytes 32 | tf_op jit(solution)/shard_map/ppermute | solution.py:17
  24.9 22.0 %collective-permute-start.13 = (f32[512,384]{1,0:T(8,128)S(1)}, f32[512,384]{1,0:T(8,128)S(1)}, u32[]{:S(2)}, u32[]{:S(2)}) collective-permute-start(f32[512,384]{1,0:T(8,128)S(1)} %collective-permute-done.11), channel_id=1, source_target_pairs={{0,1},{1,0},{2,3},{3,2},{4,5},{5,4},{6,7},{7,6},{8,9},{9,8},{10,11... | collective-permute-start | bytes 2359304 | tf_op jit(solution)/shard_map/ppermute | solution.py:17
  44.4 28.8 %collective-permute-start.14 = (f32[512,384]{1,0:T(8,128)}, f32[512,384]{1,0:T(8,128)S(1)}, u32[]{:S(2)}, u32[]{:S(2)}) collective-permute-start(f32[512,384]{1,0:T(8,128)} %collective-permute-done.12), channel_id=1, source_target_pairs={{0,1},{1,0},{2,3},{3,2},{4,5},{5,4},{6,7},{7,6},{8,9},{9,8},{10,11... | collective-permute-start | bytes 2359304 | tf_op jit(solution)/shard_map/ppermute | solution.py:17
  51.2 9.9 %collective-permute-start.15 = (f32[192,384]{1,0:T(8,128)S(1)}, f32[192,384]{1,0:T(8,128)S(1)}, u32[]{:S(2)}, u32[]{:S(2)}) collective-permute-start(f32[192,384]{1,0:T(8,128)S(1)} %get-tuple-element.21), channel_id=1, source_target_pairs={{0,4},{1,5},{2,6},{3,7},{4,0},{5,1},{6,2},{7,3},{8,12},{9,13},{10,... | collective-permute-start | bytes 884744 | tf_op jit(solution)/shard_map/ppermute | solution.py:17
  53.0 15.2 %collective-permute-start.16 = (f32[192,384]{1,0:T(8,128)S(1)}, f32[192,384]{1,0:T(8,128)S(1)}, u32[]{:S(2)}, u32[]{:S(2)}) collective-permute-start(f32[192,384]{1,0:T(8,128)S(1)} %get-tuple-element.23), channel_id=1, source_target_pairs={{0,2},{1,3},{2,0},{3,1},{4,6},{5,7},{6,4},{7,5},{8,10},{9,11},{10,... | collective-permute-start | bytes 884744 | tf_op jit(solution)/shard_map/ppermute | solution.py:17
  54.5 14.2 %collective-permute-start.17 = (f32[192,384]{1,0:T(8,128)S(1)}, f32[192,384]{1,0:T(8,128)S(1)}, u32[]{:S(2)}, u32[]{:S(2)}) collective-permute-start(f32[192,384]{1,0:T(8,128)S(1)} %get-tuple-element.22), channel_id=1, source_target_pairs={{0,6},{1,7},{2,4},{3,5},{4,2},{5,3},{6,0},{7,1},{8,14},{9,15},{10,... | collective-permute-start | bytes 884744 | tf_op jit(solution)/shard_map/ppermute | solution.py:17
  58.6 25.1 %collective-permute-start.1 = (f32[288,384]{1,0:T(8,128)S(1)}, f32[288,384]{1,0:T(8,128)S(1)}, u32[]{:S(2)}, u32[]{:S(2)}) collective-permute-start(f32[288,384]{1,0:T(8,128)S(1)} %dynamic-slice_bitcast_fusion.3), channel_id=1, source_target_pairs={{0,4},{1,5},{2,6},{3,7},{4,0},{5,1},{6,2},{7,3},{8,12},{9,13},{10,... | collective-permute-start | bytes 1327112 | tf_op jit(solution)/shard_map/ppermute | solution.py:17
  68.8 5.7 %collective-permute-start.18 = (f32[48,384]{1,0:T(8,128)S(1)}, f32[48,384]{1,0:T(8,128)S(1)}, u32[]{:S(2)}, u32[]{:S(2)}) collective-permute-start(f32[48,384]{1,0:T(8,128)S(1)} %get-tuple-element.27), channel_id=1, source_target_pairs={{0,8},{1,9},{2,10},{3,11},{4,12},{5,13},{6,14},{7,15},{8,0},{9,1},... | collective-permute-start | bytes 221192 | tf_op jit(solution)/shard_map/ppermute | solution.py:17
  70.4 7.1 %collective-permute-start.19 = (f32[48,384]{1,0:T(8,128)S(1)}, f32[48,384]{1,0:T(8,128)S(1)}, u32[]{:S(2)}, u32[]{:S(2)}) collective-permute-start(f32[48,384]{1,0:T(8,128)S(1)} %get-tuple-element.29), channel_id=1, source_target_pairs={{0,16},{1,17},{2,18},{3,19},{4,20},{5,21},{6,22},{7,23},{8,24},{9,... | collective-permute-start | bytes 221192 | tf_op jit(solution)/shard_map/ppermute | solution.py:17
  73.0 6.2 %collective-permute-start.20 = (f32[48,384]{1,0:T(8,128)S(1)}, f32[48,384]{1,0:T(8,128)S(1)}, u32[]{:S(2)}, u32[]{:S(2)}) collective-permute-start(f32[48,384]{1,0:T(8,128)S(1)} %get-tuple-element.28), channel_id=1, source_target_pairs={{0,24},{1,25},{2,26},{3,27},{4,28},{5,29},{6,30},{7,31},{8,16},{9,... | collective-permute-start | bytes 221192 | tf_op jit(solution)/shard_map/ppermute | solution.py:17
  79.3 6.8 %collective-permute-start.22 = (f32[48,384]{1,0:T(8,128)S(1)}, f32[48,384]{1,0:T(8,128)S(1)}, u32[]{:S(2)}, u32[]{:S(2)}) collective-permute-start(f32[48,384]{1,0:T(8,128)S(1)} %get-tuple-element.8), channel_id=1, source_target_pairs={{0,8},{1,9},{2,10},{3,11},{4,12},{5,13},{6,14},{7,15},{8,0},{9,1},... | collective-permute-start | bytes 221192 | tf_op jit(solution)/shard_map/ppermute | solution.py:17
  79.3 8.9 %collective-permute-start.23 = (f32[48,384]{1,0:T(8,128)S(1)}, f32[48,384]{1,0:T(8,128)S(1)}, u32[]{:S(2)}, u32[]{:S(2)}) collective-permute-start(f32[48,384]{1,0:T(8,128)S(1)} %get-tuple-element.8), channel_id=1, source_target_pairs={{0,16},{1,17},{2,18},{3,19},{4,20},{5,21},{6,22},{7,23},{8,24},{9,... | collective-permute-start | bytes 221192 | tf_op jit(solution)/shard_map/ppermute | solution.py:17
  81.5 7.1 %collective-permute-start.24 = (f32[48,384]{1,0:T(8,128)S(1)}, f32[48,384]{1,0:T(8,128)S(1)}, u32[]{:S(2)}, u32[]{:S(2)}) collective-permute-start(f32[48,384]{1,0:T(8,128)S(1)} %get-tuple-element.8), channel_id=1, source_target_pairs={{0,24},{1,25},{2,26},{3,27},{4,28},{5,29},{6,30},{7,31},{8,16},{9,... | collective-permute-start | bytes 221192 | tf_op jit(solution)/shard_map/ppermute | solution.py:17
  83.8 6.9 %collective-permute-start.2 = (f32[72,384]{1,0:T(8,128)S(1)}, f32[72,384]{1,0:T(8,128)S(1)}, u32[]{:S(2)}, u32[]{:S(2)}) collective-permute-start(f32[72,384]{1,0:T(8,128)S(1)} %get-tuple-element.24), channel_id=1, source_target_pairs={{0,8},{1,9},{2,10},{3,11},{4,12},{5,13},{6,14},{7,15},{8,0},{9,1},... | collective-permute-start | bytes 331784 | tf_op jit(solution)/shard_map/ppermute | solution.py:17
  83.9 12.3 %collective-permute-start.3 = (f32[72,384]{1,0:T(8,128)S(1)}, f32[72,384]{1,0:T(8,128)S(1)}, u32[]{:S(2)}, u32[]{:S(2)}) collective-permute-start(f32[72,384]{1,0:T(8,128)S(1)} %get-tuple-element.26), channel_id=1, source_target_pairs={{0,16},{1,17},{2,18},{3,19},{4,20},{5,21},{6,22},{7,23},{8,24},{9,... | collective-permute-start | bytes 331784 | tf_op jit(solution)/shard_map/ppermute | solution.py:17
  86.1 10.1 %collective-permute-start.4 = (f32[72,384]{1,0:T(8,128)S(1)}, f32[72,384]{1,0:T(8,128)S(1)}, u32[]{:S(2)}, u32[]{:S(2)}) collective-permute-start(f32[72,384]{1,0:T(8,128)S(1)} %get-tuple-element.25), channel_id=1, source_target_pairs={{0,24},{1,25},{2,26},{3,27},{4,28},{5,29},{6,30},{7,31},{8,16},{9,... | collective-permute-start | bytes 331784 | tf_op jit(solution)/shard_map/ppermute | solution.py:17
  88.6 24.9 %collective-permute-start.25 = (f32[192,384]{1,0:T(8,128)S(1)}, f32[192,384]{1,0:T(8,128)S(1)}, u32[]{:S(2)}, u32[]{:S(2)}) collective-permute-start(f32[192,384]{1,0:T(8,128)S(1)} %bitcast.183), channel_id=1, source_target_pairs={{0,4},{1,5},{2,6},{3,7},{4,0},{5,1},{6,2},{7,3},{8,12},{9,13},{10,... | collective-permute-start | bytes 884744 | tf_op jit(solution)/shard_map/ppermute | solution.py:17
  90.1 23.4 %collective-permute-start.26 = (f32[192,384]{1,0:T(8,128)S(1)}, f32[192,384]{1,0:T(8,128)S(1)}, u32[]{:S(2)}, u32[]{:S(2)}) collective-permute-start(f32[192,384]{1,0:T(8,128)S(1)} %bitcast.184), channel_id=1, source_target_pairs={{0,2},{1,3},{2,0},{3,1},{4,6},{5,7},{6,4},{7,5},{8,10},{9,11},{10,... | collective-permute-start | bytes 884744 | tf_op jit(solution)/shard_map/ppermute | solution.py:17
  90.7 22.9 %collective-permute-start.27 = (f32[192,384]{1,0:T(8,128)S(1)}, f32[192,384]{1,0:T(8,128)S(1)}, u32[]{:S(2)}, u32[]{:S(2)}) collective-permute-start(f32[192,384]{1,0:T(8,128)S(1)} %bitcast.185), channel_id=1, source_target_pairs={{0,6},{1,7},{2,4},{3,5},{4,2},{5,3},{6,0},{7,1},{8,14},{9,15},{10,... | collective-permute-start | bytes 884744 | tf_op jit(solution)/shard_map/ppermute | solution.py:17
  97.8 5.9 %collective-permute-start.6 = (f32[72,384]{1,0:T(8,128)S(1)}, f32[72,384]{1,0:T(8,128)S(1)}, u32[]{:S(2)}, u32[]{:S(2)}) collective-permute-start(f32[72,384]{1,0:T(8,128)S(1)} %get-tuple-element.6), channel_id=1, source_target_pairs={{0,8},{1,9},{2,10},{3,11},{4,12},{5,13},{6,14},{7,15},{8,0},{9,1},... | collective-permute-start | bytes 331784 | tf_op jit(solution)/shard_map/ppermute | solution.py:17
  100.0 9.2 %collective-permute-start.7 = (f32[72,384]{1,0:T(8,128)S(1)}, f32[72,384]{1,0:T(8,128)S(1)}, u32[]{:S(2)}, u32[]{:S(2)}) collective-permute-start(f32[72,384]{1,0:T(8,128)S(1)} %get-tuple-element.6), channel_id=1, source_target_pairs={{0,16},{1,17},{2,18},{3,19},{4,20},{5,21},{6,22},{7,23},{8,24},{9,... | collective-permute-start | bytes 331784 | tf_op jit(solution)/shard_map/ppermute | solution.py:17
  103.7 6.7 %collective-permute-start.8 = (f32[72,384]{1,0:T(8,128)S(1)}, f32[72,384]{1,0:T(8,128)S(1)}, u32[]{:S(2)}, u32[]{:S(2)}) collective-permute-start(f32[72,384]{1,0:T(8,128)S(1)} %get-tuple-element.6), channel_id=1, source_target_pairs={{0,24},{1,25},{2,26},{3,27},{4,28},{5,29},{6,30},{7,31},{8,16},{9,... | collective-permute-start | bytes 331784 | tf_op jit(solution)/shard_map/ppermute | solution.py:17
  111.0 8.8 %collective-permute-start.9 = (f32[288,384]{1,0:T(8,128)}, f32[288,384]{1,0:T(8,128)}, u32[]{:S(2)}, u32[]{:S(2)}) collective-permute-start(f32[288,384]{1,0:T(8,128)} %bitcast.19), channel_id=1, source_target_pairs={{0,4},{1,5},{2,6},{3,7},{4,0},{5,1},{6,2},{7,3},{8,12},{9,13},{10,... | collective-permute-start | bytes 1327112 | tf_op jit(solution)/shard_map/ppermute | solution.py:17
  113.5 0.9 copy-start.11
  115.3 11.5 %collective-permute-start.28 = (f32[384,384]{1,0:T(8,128)}, f32[384,384]{1,0:T(8,128)}, u32[]{:S(2)}, u32[]{:S(2)}) collective-permute-start(f32[384,384]{1,0:T(8,128)} %dynamic-slice_bitcast_fusion.2), channel_id=1, source_target_pairs={{0,1},{1,0},{2,3},{3,2},{4,5},{5,4},{6,7},{7,6},{8,9},{9,8},{10,11... | collective-permute-start | bytes 1769480 | tf_op jit(solution)/shard_map/ppermute | solution.py:17
  117.2 5.7 %copy-start.1 = (f32[1024,1,384]{2,1,0:T(1,128)S(1)}, f32[1024,1,384]{2,1,0:T(1,128)}, u32[]{:S(2)}) copy-start(f32[1024,1,384]{2,1,0:T(1,128)} %param.4) | copy-start | bytes 4718596
  122.6 4.3 %copy-start.2 = (f32[512,384]{1,0:T(8,128)S(1)}, f32[512,384]{1,0:T(8,128)}, u32[]{:S(2)}) copy-start(f32[512,384]{1,0:T(8,128)} %get-tuple-element.11) | copy-start | bytes 2359300
  122.6 4.2 %copy-start.4 = (f32[512,384]{1,0:T(8,128)S(1)}, f32[512,384]{1,0:T(8,128)}, u32[]{:S(2)}) copy-start(f32[512,384]{1,0:T(8,128)} %get-tuple-element.12) | copy-start | bytes 2359300
  122.6 4.2 %copy-start.6 = (f32[512,384]{1,0:T(8,128)S(1)}, f32[512,384]{1,0:T(8,128)}, u32[]{:S(2)}) copy-start(f32[512,384]{1,0:T(8,128)} %get-tuple-element.13) | copy-start | bytes 2359300
  122.6 4.2 %copy-start.8 = (f32[512,384]{1,0:T(8,128)S(1)}, f32[512,384]{1,0:T(8,128)}, u32[]{:S(2)}) copy-start(f32[512,384]{1,0:T(8,128)} %get-tuple-element.14) | copy-start | bytes 2359300
  122.6 4.2 %copy-start.13 = (f32[384,384]{0,1:T(8,128)S(1)}, f32[384,384]{0,1:T(8,128)}, u32[]{:S(2)}) copy-start(f32[384,384]{0,1:T(8,128)} %copy.28) | copy-start | bytes 1769476
  122.6 6.9 %collective-permute-start.10 = (f32[192,384]{1,0:T(8,128)S(1)}, f32[192,384]{1,0:T(8,128)S(1)}, u32[]{:S(2)}, u32[]{:S(2)}) collective-permute-start(f32[192,384]{1,0:T(8,128)S(1)} %slice.39), channel_id=1, source_target_pairs={{0,1},{1,0},{2,3},{3,2},{4,5},{5,4},{6,7},{7,6},{8,9},{9,8},{10,11... | collective-permute-start | bytes 884744 | tf_op jit(solution)/shard_map/ppermute | solution.py:17
  131.4 5.5 %copy-start.10 = (f32[384,1024]{1,0:T(8,128)S(1)}, f32[384,1024]{1,0:T(8,128)}, u32[]{:S(2)}) copy-start(f32[384,1024]{1,0:T(8,128)} %fusion.18) | copy-start | bytes 4718596
  133.6 3.2 %copy-start.3 = (f32[512,384]{1,0:T(8,128)S(1)}, f32[512,384]{1,0:T(8,128)}, u32[]{:S(2)}) copy-start(f32[512,384]{1,0:T(8,128)} %get-tuple-element.11) | copy-start | bytes 2359300
  133.6 3.2 %copy-start.5 = (f32[512,384]{1,0:T(8,128)S(1)}, f32[512,384]{1,0:T(8,128)}, u32[]{:S(2)}) copy-start(f32[512,384]{1,0:T(8,128)} %get-tuple-element.12) | copy-start | bytes 2359300
  133.6 3.2 %copy-start.7 = (f32[512,384]{1,0:T(8,128)S(1)}, f32[512,384]{1,0:T(8,128)}, u32[]{:S(2)}) copy-start(f32[512,384]{1,0:T(8,128)} %get-tuple-element.13) | copy-start | bytes 2359300
  133.6 3.3 %copy-start.9 = (f32[512,384]{1,0:T(8,128)S(1)}, f32[512,384]{1,0:T(8,128)}, u32[]{:S(2)}) copy-start(f32[512,384]{1,0:T(8,128)} %get-tuple-element.14) | copy-start | bytes 2359300
  133.6 3.3 %copy-start.12 = (f32[384,384]{0,1:T(8,128)S(1)}, f32[384,384]{0,1:T(8,128)}, u32[]{:S(2)}) copy-start(f32[384,384]{0,1:T(8,128)} %copy.30) | copy-start | bytes 1769476
